TPU v7x, 32 devices: a whole 2x2x4 slice. The times are simulated.
32 devices in a mesh: tm: 16 (over z, y, x), seq: 2 (over core).
Axes of the slice: x: 2, y: 2, z: 4, core: 2. Of those that a mesh axis runs over, the one named last changes fastest.
Arguments:
- gains: float32 [128, 128, 128], P(('seq', 'tm')), parts along dimension 0, may hold values from -1 to 1
- offsets: float32 [128, 128], P(('seq', 'tm')), parts along dimension 0, may hold values from -8 to 8
- cov_terms: float32 [128, 128, 128], P(('seq', 'tm')), parts along dimension 0, as said below
Outputs:
- smoothed_means: float32 [128, 128], P(('seq', 'tm')), parts along dimension 0
- smoothed_covs: float32 [128, 128, 128], P(('seq', 'tm')), parts along dimension 0
- moments: float32 [256, 128], P('seq'), parts along dimension 0
There are 2 independent parts, one for each index of `seq`. A program takes and returns all parts, laid end to end along the dimension named above; each array names one. Nothing has to cross between parts.
Inputs may be any that keep to these rules, and one draw needn't show every extreme that they name: `cov_terms`: each step's covariance term is symmetric positive definite.
All inputs are finite; a program needn't handle non-finite values.
Results may differ from a plain program's by a relative error of at most 0.00014.
Values sent between devices are 32-bit elements; how exact they have to be, the bound alone decides.
A program may use at most 128 MiB of HBM per device.

v0:
```python
import jax
import jax.numpy as jnp
from jax import lax
from jax.sharding import PartitionSpec as P


def prefix(part, axis, combine, identity):
    count = lax.axis_size(axis)
    place = lax.axis_index(axis)
    ahead = count - 1 - place
    gathered = jax.tree.map(lambda a: lax.all_gather(a, axis), part)
    state = jax.tree.map(lambda a, e: jnp.zeros_like(a) + jnp.asarray(e, a.dtype), part, identity)

    def one(lap, state):
        source = count - 1 - lap
        return combine(
            state, jax.tree.map(lambda a: lax.dynamic_index_in_dim(a, source, 0, False), gathered)
        )

    return lax.fori_loop(0, ahead, one, state)


def product(left, right):
    return jnp.dot(left, right, precision=lax.Precision.HIGHEST, preferred_element_type=jnp.float32)


def compose(earlier, following):
    gain_left, offset_left, prior_spread_matrix = earlier
    gain_right, offset_right, cov_right = following
    gain = product(gain_left, gain_right)
    offset = offset_left + product(gain_left, offset_right)
    covariance = prior_spread_matrix + product(product(gain_left, cov_right), gain_left.T)
    return (gain, offset, covariance)


def join_higher(higher, lower):
    return compose(lower, higher)


def drop_suffix(boundary, element):
    merged = compose(element, boundary)
    return (merged, None)


def walk(state_pair, element):
    upcoming_average, cov_next = state_pair
    gain, offset, covariance = element
    mean_now = offset + product(gain, upcoming_average)
    cov_now = covariance + product(product(gain, cov_next), gain.T)
    return ((mean_now, cov_now), (mean_now, cov_now))


def local(gains, offsets, cov_terms):
    devices = lax.axis_size("tm")
    position = lax.axis_index("tm")
    local_steps = gains.shape[0]
    width = gains.shape[1]
    final_step = jnp.logical_and(
        jnp.arange(local_steps) == local_steps - 1, position == devices - 1
    )
    gains = jnp.where(final_step[:, None, None], jnp.zeros_like(gains), gains)
    unit = (
        jnp.eye(width, dtype=jnp.float32),
        jnp.zeros((width,), jnp.float32),
        jnp.zeros((width, width), jnp.float32),
    )
    aggregate, unused = lax.scan(drop_suffix, unit, (gains, offsets, cov_terms), reverse=True)
    boundary = prefix((aggregate[0], aggregate[1], aggregate[2]), "tm", join_higher, unit)
    final_pair, outputs = lax.scan(
        walk, (boundary[1], boundary[2]), (gains, offsets, cov_terms), reverse=True
    )
    mean_rows, cov_rows = outputs
    local_moment = jnp.sum(cov_rows, axis=0) + product(mean_rows.T, mean_rows)
    total_moment = lax.psum(local_moment, "tm")
    moments = total_moment / (local_steps * devices)
    return (mean_rows, cov_rows, moments)


def solution(mesh):
    in_specs = (P(("seq", "tm"), None, None), P(("seq", "tm"), None), P(("seq", "tm"), None, None))
    out_specs = (P(("seq", "tm"), None), P(("seq", "tm"), None, None), P("seq", None))
    return jax.shard_map(local, mesh=mesh, in_specs=in_specs, out_specs=out_specs, check_vma=False)
```

profile of v0, /device:TPU:0, one launch (start us, length us, event | category | flops | bytes accessed | tf_op | source)
XLA Modules:
  0.0 288.2 jit_solution(3906093262499196804)
XLA Ops:
  8.4 3.9 %while.57 = (s32[]{:T(128)}, f32[128,128]{1,0:T(8,128)S(1)}, f32[128]{0:T(128)S(1)}, f32[128,128]{1,0:T(8,128)S(1)}, f32[4,128,128]{2,1,0:T(8,128)S(1)}, /*index...) while((s32[]{:T(128)}, f32[128,128]{1,0:T(8,128)S(1)}, ...), condition=%wide.region_1.2_spmd.clone, body=%wide.region_0.1_spmd.clone.sunk | while | flops 75727104 | bytes 857219 | solution.py:67
  13.7 42.2 %all-gather.3 = f32[16,1,128]{2,1,0:T(1,128)S(1)} all-gather(f32[1,1,128]{2,1,0:T(1,128)S(1)} %bitcast.141), channel_id=2, replica_groups=mesh['tm'=16,'seq'=2] {'tm'}, dimensions={0}, use_global_device_ids=true | all-gather | bytes 8704 | tf_op jit(solution)/shard_map/all_gather | solution.py:11
  55.9 15.2 %all-gather.7.cloned.1.call-done = f32[2048,128]{1,0:T(8,128)} async-done(((f32[128,128]{1,0:T(8,128)}), f32[2048,128]{1,0:T(8,128)}) %all-gather.7.cloned.1.call-update) | async-done | bytes 1048592 | tf_op jit(solution)/shard_map/all_gather | solution.py:11
  71.1 57.4 %all-gather.9.cloned.1.call-done = f32[2048,128]{1,0:T(8,128)} async-done(((f32[128,128]{1,0:T(8,128)}), f32[2048,128]{1,0:T(8,128)}) %all-gather.9.cloned.1.call-update) | async-done | bytes 1048592 | tf_op jit(solution)/shard_map/all_gather | solution.py:11
  128.5 49.0 %while.55 = (s32[]{:T(128)}, f32[128]{0:T(128)S(1)}, f32[128,128]{1,0:T(8,128)S(1)}, s32[]{:T(128)}, f32[16,128]{1,0:T(8,128)S(1)}, /*index=5*/f32[16,128,128]{2...) while((s32[]{:T(128)}, f32[128]{0:T(128)S(1)}, ...), condition=%wide.region_3.4_spmd, body=%wide.region_2.3_spmd.sunk | while | flops 50544772 | bytes 529055 | solution.py:20
  129.6 1.1 convolution_add_fusion.6
  132.8 1.1 convolution_add_fusion.6
  136.1 1.1 convolution_add_fusion.6
  139.4 1.1 convolution_add_fusion.6
  142.7 1.1 convolution_add_fusion.6
  145.9 1.1 convolution_add_fusion.6
  149.2 1.1 convolution_add_fusion.6
  152.5 1.1 convolution_add_fusion.6
  155.7 1.1 convolution_add_fusion.6
  159.0 1.1 convolution_add_fusion.6
  162.3 1.1 convolution_add_fusion.6
  164.5 1.1 fusion.92
  165.6 1.1 convolution_add_fusion.6
  168.8 1.1 convolution_add_fusion.6
  172.1 1.1 convolution_add_fusion.6
  175.4 1.1 convolution_add_fusion.6
  177.6 3.0 %while.56 = (s32[]{:T(128)}, f32[128]{0:T(128)S(1)}, f32[128,128]{1,0:T(8,128)S(1)}, f32[4,128]{1,0:T(4,128)S(1)}, f32[4,128,128]{2,1,0:T(8,128)S(1)}, /*index=5...) while((s32[]{:T(128)}, f32[128]{0:T(128)S(1)}, ...), condition=%wide.region_5.6_spmd, body=%wide.region_4.5_spmd.sunk | while | flops 50544768 | bytes 595585 | solution.py:69
  182.2 98.0 %all-reduce.2.cloned.1.call-done = f32[128,128]{1,0:T(8,128)} async-done(((f32[128,128]{1,0:T(8,128)}), f32[128,128]{1,0:T(8,128)}) %all-reduce.2.cloned.1.call-update) | async-done | bytes 65552 | tf_op jit(solution)/shard_map/psum | solution.py:74
  280.2 1.5 broadcast_multiply_fusion
  (117 shorter events, 41.2 us)
Async XLA Ops:
  7.2 63.9 %all-gather.7.cloned.1.call-start = ((), (), s32[]{:S(2)}) async-start(), calls=%async_computation.1 | async-start | bytes 1114112 | tf_op jit(solution)/shard_map/all_gather | solution.py:11
  7.3 1.1 copy-start.2
  7.3 1.1 copy-start.5
  12.3 0.6 copy-start
  12.3 0.7 copy-start.1
  12.9 115.6 %all-gather.9.cloned.1.call-start = ((), (), s32[]{:S(2)}) async-start(), calls=%async_computation.2 | async-start | bytes 1114112 | tf_op jit(solution)/shard_map/all_gather | solution.py:11
  13.7 266.5 %all-reduce.2.cloned.1.call-start = ((), (), s32[]{:S(2)}) async-start(), calls=%async_computation | async-start | bytes 131072 | tf_op jit(solution)/shard_map/psum | solution.py:74
  180.7 0.6 copy-start.4
  180.7 1.5 copy-start.3
Sparse Core Ops, SparseCore 0:
  13.0 57.9 all-gather.6
  74.4 54.0 all-gather.8
  182.3 97.8 all-reduce.1
where the time goes:
time: 291 us; the launch traced here: 288 us
  waiting for transfers between devices  171 us (59%)
  matrix products  55.8 us (19%)
  blocking collectives  42.2 us (15%)
  between operations  13.9 us (5%)
    psum x1, waiting for transfers between devices, local(): total_moment = lax.psum(local_moment, 'tm')  98 us
    all_gather x2, waiting for transfers between devices, prefix(): gathered = jax.tree.map(lambda a: lax.all_gather(a, axis), part)  72.6 us
    dot_general x74, matrix products, product(): jnp.dot(left, right, precision=lax.Precision.HIGHEST, preferred_element_t...  55.8 us
    all_gather x1, blocking collectives, prefix(): gathered = jax.tree.map(lambda a: lax.all_gather(a, axis), part)  42.2 us
  transfers between devices with their start and end apart: 3, of which 3 were waited for; matrix products, arithmetic and copies ran while one was open for 0% of the time, Pallas kernels for 0%

commit v1 on v0

v1 whole, which is shorter than its diff:
```python
import functools

import jax
import jax.numpy as jnp
from jax import lax
from jax.experimental import pallas as pl
from jax.experimental.pallas import tpu as pltpu
from jax.sharding import PartitionSpec as P

F32 = jnp.float32
BF16 = jnp.bfloat16
GROUP = 16


def split(x):
    hi = x.astype(BF16)
    return hi, (x - hi.astype(F32)).astype(BF16)


def left(x):
    hi, lo = split(x)
    return hi, jnp.concatenate([hi, lo], axis=1)


def right(w):
    hi, lo = split(w)
    return jnp.concatenate([hi, hi], axis=0), lo


def mul(x, w):
    hi, both = x
    w_hi, w_lo = w
    return jnp.dot(both, w_hi, preferred_element_type=F32) + jnp.dot(
        hi, w_lo, preferred_element_type=F32
    )


def kernel(
    n, gains, offsets, covs, means_out, covs_out, mom_out,
    psi, mp, snd_psi, snd_mp, rcv_psi, rcv_mp, mom, rs_buf, red, bf_snd, bf_rcv, mom_all,
    ps_s, ps_r, mp_s, mp_r, rs_s, rs_r, bf_s, bf_r, ag_s, ag_r, out_s,
):
    steps, width = gains.shape[0], gains.shape[1]
    me = lax.axis_index("tm")
    rounds = n.bit_length() - 3
    quarter = n // 4
    place = lax.rem(me, GROUP)
    base = me - place
    rows = width // GROUP
    wide = n // GROUP

    def flip(step):
        bit = lax.rem(lax.div(me, step), 2)
        return me + step * (1 - 2 * bit), bit

    peers = [base + lax.rem(place + j, GROUP) for j in range(1, GROUP)]
    far = GROUP
    while far < n:
        peers.append(flip(far)[0])
        far *= 2
    q = lax.div(me, quarter)
    if n > GROUP:
        peers.append(lax.rem(me, quarter) + quarter * (3 - q))
    barrier = pltpu.get_barrier_semaphore()
    for peer in peers:
        pl.semaphore_signal(barrier, inc=1, device_id={"tm": peer}, device_id_type=pl.DeviceIdType.MESH)

    def send(src, dst, s, r, to):
        return pltpu.make_async_remote_copy(
            src_ref=src, dst_ref=dst, send_sem=s, recv_sem=r,
            device_id={"tm": to}, device_id_type=pl.DeviceIdType.MESH,
        )

    for t in reversed(range(steps)):
        gain = gains[t]
        if t == steps - 1:
            gain = jnp.where(me == n - 1, jnp.zeros_like(gain), gain)
        gain_t = gain.T
        offset = jnp.broadcast_to(offsets[t : t + 1, :], (8, width))
        if t == steps - 1:
            psi[t] = gain_t
            mp[t, :width] = covs[t]
            mp[t, width:] = offset
        else:
            x = mul(left(jnp.concatenate([psi[t + 1], mp[t + 1]], axis=0)), right(gain_t))
            psi[t] = x[:width]
            mp[t, width:] = x[2 * width :] + offset
            mp[t, :width] = covs[t] + mul(left(gain), right(x[width : 2 * width]))

    def compose(e_psi, e_mp, f_psi, f_mp):
        parts = [f_mp] if f_psi is None else [f_mp, f_psi]
        x = mul(left(jnp.concatenate(parts, axis=0)), right(e_psi))
        p = e_mp[:width] + mul(left(e_psi.T), right(x[:width]))
        m = e_mp[width:] + x[width : width + 8]
        return (None if f_psi is None else x[width + 8 :]), p, m

    def absorb(slot, with_gain):
        f_psi = rcv_psi[slot] if with_gain else None
        for t in range(steps):
            new_psi, p, m = compose(psi[t], mp[t], f_psi, rcv_mp[slot])
            if with_gain:
                psi[t] = new_psi
            mp[t, :width] = p
            mp[t, width:] = m

    pl.semaphore_wait(barrier, len(peers))

    snd_psi[0] = psi[0]
    snd_mp[0] = mp[0]
    waits = []
    for k in range(rounds):
        to, bit = flip(1 << k)
        a = send(snd_psi.at[k], rcv_psi.at[k], ps_s.at[k], ps_r.at[k], to)
        b = send(snd_mp.at[k], rcv_mp.at[k], mp_s.at[k], mp_r.at[k], to)
        a.start()
        b.start()
        waits += [a, b]
        if k:
            @pl.when(lax.rem(lax.div(me, 1 << (k - 1)), 2) == 0)
            def _():
                absorb(k - 1, True)
        a.wait_recv()
        b.wait_recv()
        upper = bit == 1
        own_psi, own_mp, got_psi, got_mp = snd_psi[k], snd_mp[k], rcv_psi[k], rcv_mp[k]
        e_psi = jnp.where(upper, got_psi, own_psi)
        f_psi = jnp.where(upper, own_psi, got_psi)
        e_mp = jnp.where(upper, got_mp, own_mp)
        f_mp = jnp.where(upper, own_mp, got_mp)
        new_psi, p, m = compose(e_psi, e_mp, f_psi, f_mp)
        snd_psi[k + 1] = new_psi
        snd_mp[k + 1, :width] = p
        snd_mp[k + 1, width:] = m

    def settle():
        @pl.when(lax.rem(lax.div(me, 1 << (rounds - 1)), 2) == 0)
        def _():
            absorb(rounds - 1, True)

    one, two = rounds, rounds + 1
    down, down2 = lax.rem(me + n - quarter, n), lax.rem(me + n - 2 * quarter, n)
    near_mp = send(snd_mp.at[one], rcv_mp.at[one], mp_s.at[one], mp_r.at[one], down)
    near_psi = send(snd_psi.at[one], rcv_psi.at[one], ps_s.at[one], ps_r.at[one], down)
    top_far = send(snd_mp.at[two], rcv_mp.at[two], mp_s.at[two], mp_r.at[two], down2)
    top_near = send(snd_mp.at[two], rcv_mp.at[two], mp_s.at[two + 1], mp_r.at[two], down)

    @pl.when(q == 3)
    def _():
        near_mp.start()
        settle()
        near_mp.wait_send()

    @pl.when(q == 2)
    def _():
        near_mp.wait_recv()
        unused, p, m = compose(snd_psi[one], snd_mp[one], None, rcv_mp[one])
        snd_mp[two, :width] = p
        snd_mp[two, width:] = m
        top_far.start()
        top_near.start()
        settle()
        absorb(one, False)
        top_far.wait_send()
        top_near.wait_send()

    @pl.when(q == 1)
    def _():
        near_psi.start()
        near_mp.start()
        settle()
        top_near.wait_recv()
        absorb(two, False)
        near_psi.wait_send()
        near_mp.wait_send()

    @pl.when(q == 0)
    def _():
        settle()
        near_psi.wait_recv()
        near_mp.wait_recv()
        absorb(one, True)
        top_far.wait_recv()
        absorb(two, False)

    out_copies = []
    for t in range(steps):
        c = pltpu.make_async_copy(mp.at[t, pl.ds(0, width)], covs_out.at[t], out_s.at[t])
        c.start()
        out_copies.append(c)

    means = jnp.concatenate([mp[t, width : width + 1] for t in range(steps)], axis=0)
    means_out[...] = means
    total = mp[0, :width]
    for t in range(1, steps):
        total = total + mp[t, :width]
    m_hi, m_lo = split(means)
    outer = lambda u, v: lax.dot_general(u, v, (((0,), (0,)), ((), ())), preferred_element_type=F32)
    total = total + (outer(m_hi, m_hi) + (outer(m_hi, m_lo) + outer(m_lo, m_hi)))
    mom[...] = total * (1.0 / (steps * n))

    mine = pl.ds(pl.multiple_of(place * rows, rows), rows)
    scatter = []
    for j in range(1, GROUP):
        to = lax.rem(place + j, GROUP)
        c = send(
            mom.at[pl.ds(pl.multiple_of(to * rows, rows), rows)], rs_buf.at[j - 1],
            rs_s.at[j - 1], rs_r.at[j - 1], base + to,
        )
        c.start()
        scatter.append(c)
    acc = mom[mine, :]
    for j in range(1, GROUP):
        scatter[j - 1].wait_recv()
        acc = acc + rs_buf[j - 1]
    step, k = GROUP, 0
    while step < n:
        bf_snd[k] = acc
        c = send(bf_snd.at[k], bf_rcv.at[k], bf_s.at[k], bf_r.at[k], flip(step)[0])
        c.start()
        c.wait()
        acc = acc + bf_rcv[k]
        step, k = step * 2, k + 1
    red[...] = acc
    gather = []
    for j in range(1, GROUP):
        to = lax.rem(place + j, GROUP)
        c = send(red, mom_all.at[mine], ag_s.at[j - 1], ag_r.at[j - 1], base + to)
        c.start()
        gather.append(c)
    mom_all[mine, :] = acc
    for c in waits + scatter + gather:
        c.wait_send()
    for c in out_copies:
        c.wait()
    for c in gather:
        c.wait_recv()
    mom_out[...] = mom_all[...]


def local(n, gains, offsets, cov_terms):
    steps, width = gains.shape[0], gains.shape[1]
    slots = n.bit_length() - 1
    far = max(1, (n // GROUP).bit_length() - 1)
    rows = width // GROUP
    dma = pltpu.SemaphoreType.DMA
    vmem = pl.BlockSpec(memory_space=pltpu.VMEM)
    return pl.pallas_call(
        functools.partial(kernel, n),
        out_shape=(
            jax.ShapeDtypeStruct((steps, width), F32),
            jax.ShapeDtypeStruct((steps, width, width), F32),
            jax.ShapeDtypeStruct((width, width), F32),
        ),
        in_specs=[vmem] * 3,
        out_specs=(vmem, pl.BlockSpec(memory_space=pl.ANY), vmem),
        scratch_shapes=[
            pltpu.VMEM((steps, width, width), F32),
            pltpu.VMEM((steps, width + 8, width), F32),
            pltpu.VMEM((slots, width, width), F32),
            pltpu.VMEM((slots, width + 8, width), F32),
            pltpu.VMEM((slots, width, width), F32),
            pltpu.VMEM((slots, width + 8, width), F32),
            pltpu.VMEM((width, width), F32),
            pltpu.VMEM((GROUP - 1, rows, width), F32),
            pltpu.VMEM((rows, width), F32),
            pltpu.VMEM((far, rows, width), F32),
            pltpu.VMEM((far, rows, width), F32),
            pltpu.VMEM((width, width), F32),
            dma((slots,)), dma((slots,)), dma((slots + 1,)), dma((slots,)),
            dma((GROUP - 1,)), dma((GROUP - 1,)),
            dma((far,)), dma((far,)),
            dma((GROUP - 1,)), dma((GROUP - 1,)),
            dma((steps,)),
        ],
        compiler_params=pltpu.CompilerParams(collective_id=0, has_side_effects=True),
    )(gains, offsets, cov_terms)


def solution(mesh):
    n = mesh.shape["tm"]
    in_specs = (P(("seq", "tm"), None, None), P(("seq", "tm"), None), P(("seq", "tm"), None, None))
    out_specs = (P(("seq", "tm"), None), P(("seq", "tm"), None, None), P("seq", None))
    return jax.shard_map(
        functools.partial(local, n), mesh=mesh, in_specs=in_specs, out_specs=out_specs, check_vma=False
    )
```

time: 291 us -> 39.6 us (0.14)
  waiting for transfers between devices: 171 us -> 0 us
  matrix products: 55.8 us -> 0 us
  blocking collectives: 42.2 us -> 0 us
  Pallas kernels: 0 us -> 35.2 us
  between operations: 13.9 us -> 0.65 us
    psum x1 -> x0, waiting for transfers between devices: 98 us -> none  [local(): total_moment = lax.psum(local_moment, 'tm')]
    all_gather x2 -> x0, waiting for transfers between devices: 72.6 us -> none  [prefix(): gathered = jax.tree.map(lambda a: lax.all_gather(a, axis), part)]
    dot_general x74 -> x0, matrix products: 55.8 us -> none  [product(): jnp.dot(left, right, precision=lax.Precision.HIGHEST, preferred_element_t...]
    all_gather x1 -> x0, blocking collectives: 42.2 us -> none  [prefix(): gathered = jax.tree.map(lambda a: lax.all_gather(a, axis), part)]
    pallas_call x0 -> x1, Pallas kernels: none -> 35.2 us  [local(): pl.pallas_call(functools.partial(kernel, n), out_shape=(jax.ShapeDtypeStr...]
  transfers between devices with their start and end apart: 3 -> 0, of which waited for: 3 -> 0; matrix products, arithmetic and copies ran while one was open for 0% -> 0% of each run, Pallas kernels for 0% -> 0%
where the time goes in v1:
time: 39.6 us; the launch traced here: 39.4 us
  Pallas kernels  35.2 us (89%)
  local copies, waits for them, and re-layouts  3.57 us (9%)
  between operations  0.65 us (2%)
    pallas_call x1, Pallas kernels, local(): pl.pallas_call(functools.partial(kernel, n), out_shape=(jax.ShapeDtypeStr...  35.2 us
    unnamed x7, local copies, waits for them, and re-layouts  3.57 us

profile of v1, /device:TPU:0, one launch (start us, length us, event | category | flops | bytes accessed | tf_op | source)
XLA Modules:
  0.0 39.4 jit_solution(5270852420600260338)
XLA Ops:
  0.6 35.2 %shard_map.58 = (f32[4,128]{1,0:T(4,128)}, f32[4,128,128]{2,1,0:T(8,128)}, f32[128,128]{1,0:T(8,128)}) custom-call(f32[4,128,128]{2,1,0:T(8,128)} %gains.1, f32[4,128]{1,0:T(4,128)} %offsets.1, f32[4,128,128]{2,1,0:T(8,128)} %covs.1), custom_call_target="tpu_custom_call" | custom-call | tf_op jit(solution)/shard_map/pallas_call | solution.py:247
  35.8 0.0 copy-start.1
  35.8 0.7 %copy-done.1 = f32[4,128]{1,0:T(4,128)S(1)} copy-done((f32[4,128]{1,0:T(4,128)S(1)}, f32[4,128]{1,0:T(4,128)}, u32[]{:S(2)}) %copy-start.1) | copy-done | bytes 2072
  36.5 0.6 %copy.9 = f32[4,128]{1,0:T(4,128)} copy(f32[4,128]{1,0:T(4,128)S(1)} %copy-done.1) | data formatting | bytes 4096
  37.1 0.0 copy-start
  37.1 1.7 %copy.10 = f32[4,128,128]{2,1,0:T(8,128)} copy(f32[4,128,128]{2,1,0:T(8,128)} %get-tuple-element.7) | data formatting | bytes 524288
  38.8 0.0 copy-done
  38.8 0.6 %copy.11 = f32[128,128]{1,0:T(8,128)} copy(f32[128,128]{1,0:T(8,128)S(1)} %copy-done) | data formatting | bytes 131072
Async XLA Ops:
  35.8 0.7 %copy-start.1 = (f32[4,128]{1,0:T(4,128)S(1)}, f32[4,128]{1,0:T(4,128)}, u32[]{:S(2)}) copy-start(f32[4,128]{1,0:T(4,128)} %get-tuple-element.6) | copy-start | bytes 6148
  37.1 1.7 %copy-start = (f32[128,128]{1,0:T(8,128)S(1)}, f32[128,128]{1,0:T(8,128)}, u32[]{:S(2)}) copy-start(f32[128,128]{1,0:T(8,128)} %get-tuple-element.8) | copy-start | bytes 196612

commit v2 on v1

v2 whole, which is shorter than its diff:
```python
import functools

import jax
import jax.numpy as jnp
from jax import lax
from jax.experimental import pallas as pl
from jax.experimental.pallas import tpu as pltpu
from jax.sharding import PartitionSpec as P

F32 = jnp.float32
BF16 = jnp.bfloat16
PAD = 8
GROUP = 16


def split(x):
    hi = x.astype(BF16)
    return hi, (x - hi.astype(F32)).astype(BF16)


def left(x):
    hi, lo = split(x)
    return hi, jnp.concatenate([hi, lo], axis=1)


def right(w):
    hi, lo = split(w)
    return jnp.concatenate([hi, hi], axis=0), lo


def mul(x, w):
    hi, both = x
    w_hi, w_lo = w
    return jnp.dot(both, w_hi, preferred_element_type=F32) + jnp.dot(
        hi, w_lo, preferred_element_type=F32
    )


def kernel(
    n, gains, offsets, covs, means_out, covs_out, mom_out,
    own, ring, suf, z_snd, z_near, top_snd, top_rcv,
    mom, rs_buf, bf_snd, bf_rcv, red, mom_all, mean_rows,
    ring_s, ring_r, z_s, z_r, rs_s, rs_r, bf_s, bf_r, ag_s, ag_r, out_s,
):
    steps, width = gains.shape[0], gains.shape[1]
    lean = width + PAD
    me = lax.axis_index("tm")
    levels = (n.bit_length() - 1) // 2
    quarter = n // 4
    rows = width // GROUP
    place = lax.rem(me, GROUP)
    base = me - place

    def flip(step):
        return me + step * (1 - 2 * lax.rem(lax.div(me, step), 2))

    def digit_of(stride):
        return lax.rem(lax.div(me, stride), 4)

    def peer(stride, j):
        digit = digit_of(stride)
        return me + stride * (lax.rem(digit + j, 4) - digit)

    peers = [base + lax.rem(place + j, GROUP) for j in range(1, GROUP)]
    peers += [peer(4**l, j) for l in range(2, levels) for j in (1, 2, 3)]
    barrier = pltpu.get_barrier_semaphore()
    for to in peers:
        pl.semaphore_signal(barrier, inc=1, device_id={"tm": to}, device_id_type=pl.DeviceIdType.MESH)

    def send(src, dst, s, r, to):
        return pltpu.make_async_remote_copy(
            src_ref=src, dst_ref=dst, send_sem=s, recv_sem=r,
            device_id={"tm": to}, device_id_type=pl.DeviceIdType.MESH,
        )

    def compose(e, f):
        e_psi = e[lean:]
        x = mul(left(f), right(e_psi))
        p = e[:width] + mul(left(e_psi.T), right(x[:width]))
        out = [p, e[width:lean] + x[width:lean]]
        if f.shape[0] > lean:
            out.append(x[lean:])
        return jnp.concatenate(out, axis=0)

    for t in reversed(range(steps)):
        gain = gains[t]
        if t == steps - 1:
            gain = jnp.where(me == n - 1, jnp.zeros_like(gain), gain)
        offset = jnp.broadcast_to(offsets[t : t + 1, :], (PAD, width))
        element = jnp.concatenate([covs[t], offset, gain.T], axis=0)
        own[t] = element if t == steps - 1 else compose(element, own[t + 1])

    def absorb(f):
        for t in range(steps):
            own[t, : f.shape[0]] = compose(own[t], f)

    pl.semaphore_wait(barrier, len(peers))

    def deferred(l):
        digit = digit_of(4**l)

        @pl.when(digit == 0)
        def _():
            suf[...] = compose(ring[l, 1], suf[...])

        @pl.when(digit == 2)
        def _():
            suf[...] = ring[l, 3]

        @pl.when(digit < 3)
        def _():
            absorb(suf[...])

    sends = []
    total = own[0]
    for l in range(levels - 1):
        digit = digit_of(4**l)
        ring[l, digit] = total
        started = []
        for j in (2, 1, 3):
            c = send(
                ring.at[l, digit], ring.at[l, digit], ring_s.at[l, j - 1], ring_r.at[l, j - 1], peer(4**l, j)
            )
            c.start()
            started.append(c)
        if l:
            deferred(l - 1)
        for j in (1, 2, 3):
            came = lax.rem(digit + 4 - j, 4)
            send(
                ring.at[l, came], ring.at[l, came], ring_s.at[l, j - 1], ring_r.at[l, j - 1], peer(4**l, j)
            ).wait_recv()
        sends += started
        high = compose(ring[l, 2], ring[l, 3])
        total = compose(compose(ring[l, 0], ring[l, 1]), high)
        suf[...] = high
    z_snd[...] = total

    q = lax.div(me, quarter)
    down, down2 = lax.rem(me + n - quarter, n), lax.rem(me + n - 2 * quarter, n)
    part = pl.ds(0, lean)
    near_full = send(z_snd, z_near, z_s.at[0], z_r.at[0], down)
    near_lean = send(z_snd.at[part], z_near.at[part], z_s.at[0], z_r.at[0], down)
    top_far = send(top_snd, top_rcv, z_s.at[1], z_r.at[1], down2)
    top_near = send(top_snd, top_rcv, z_s.at[2], z_r.at[1], down)

    @pl.when(q == 3)
    def _():
        near_lean.start()

    @pl.when(q == 1)
    def _():
        near_full.start()

    deferred(levels - 2)

    @pl.when(q == 3)
    def _():
        near_lean.wait_send()

    @pl.when(q == 2)
    def _():
        near_lean.wait_recv()
        top_snd[...] = compose(z_snd[...], z_near[part, :])
        top_far.start()
        top_near.start()
        absorb(z_near[part, :])
        top_far.wait_send()
        top_near.wait_send()

    @pl.when(q == 0)
    def _():
        near_full.wait_recv()
        absorb(z_near[...])

    @pl.when(q < 2)
    def _():
        top_near.wait_recv()
        absorb(top_rcv[...])

    @pl.when(q == 1)
    def _():
        near_full.wait_send()

    out_copies = []
    for t in range(steps):
        out_copies.append(pltpu.make_async_copy(own.at[t, pl.ds(0, width)], covs_out.at[t], out_s.at[t]))
    means = jnp.concatenate([own[t, width : width + 1] for t in range(steps)], axis=0)
    mean_rows[...] = means
    out_copies.append(pltpu.make_async_copy(mean_rows, means_out, out_s.at[steps]))
    sums = own[0, :width]
    for t in range(1, steps):
        sums = sums + own[t, :width]
    m_hi, m_lo = split(means)
    outer = lambda u, v: lax.dot_general(u, v, (((0,), (0,)), ((), ())), preferred_element_type=F32)
    sums = sums + (outer(m_hi, m_hi) + (outer(m_hi, m_lo) + outer(m_lo, m_hi)))
    mom[...] = sums * (1.0 / (steps * n))

    def group_rows(k):
        return pl.ds(pl.multiple_of(k * rows, rows), rows)

    for j in range(1, GROUP):
        to = lax.rem(place + j, GROUP)
        c = send(mom.at[group_rows(to)], rs_buf.at[j - 1], rs_s.at[j - 1], rs_r.at[j - 1], base + to)
        c.start()
        sends.append(c)
    for c in out_copies:
        c.start()
    acc = mom[group_rows(place), :]
    for c, j in zip(sends[1 - GROUP :], range(1, GROUP)):
        c.wait_recv()
        acc = acc + rs_buf[j - 1]
    k = 0
    while GROUP << k < n:
        bf_snd[k] = acc
        c = send(bf_snd.at[k], bf_rcv.at[k], bf_s.at[k], bf_r.at[k], flip(GROUP << k))
        c.start()
        c.wait()
        acc = acc + bf_rcv[k]
        k += 1
    red[...] = acc
    gather = []
    for j in range(1, GROUP):
        to = lax.rem(place + j, GROUP)
        c = send(red, mom_all.at[group_rows(place)], ag_s.at[j - 1], ag_r.at[j - 1], base + to)
        c.start()
        gather.append(c)
    mom_all[group_rows(place), :] = acc
    for c in sends + gather:
        c.wait_send()
    for c in out_copies:
        c.wait()
    for c in gather:
        c.wait_recv()
    last = pltpu.make_async_copy(mom_all, mom_out, out_s.at[steps + 1])
    last.start()
    last.wait()


def hand_over(a, b, c, a_out, b_out, c_out, sems):
    copies = [
        pltpu.make_async_copy(x, y, sems.at[i])
        for i, (x, y) in enumerate(((b, b_out), (c, c_out), (a, a_out)))
    ]
    for copy in copies:
        copy.start()
    for copy in copies:
        copy.wait()


def local(n, gains, offsets, cov_terms):
    steps, width = gains.shape[0], gains.shape[1]
    levels = (n.bit_length() - 1) // 2
    assert n == 4**levels and levels > 1
    slab, lean, rows = 2 * width + PAD, width + PAD, width // GROUP
    far = max(1, (n // GROUP).bit_length() - 1)
    dma = pltpu.SemaphoreType.DMA
    vmem = pl.BlockSpec(memory_space=pltpu.VMEM)
    any_space = pl.BlockSpec(memory_space=pl.ANY)
    shapes = (
        jax.ShapeDtypeStruct((steps, width), F32),
        jax.ShapeDtypeStruct((steps, width, width), F32),
        jax.ShapeDtypeStruct((width, width), F32),
    )
    results = pl.pallas_call(
        functools.partial(kernel, n),
        out_shape=shapes,
        in_specs=[vmem] * 3,
        out_specs=(any_space,) * 3,
        scratch_shapes=[
            pltpu.VMEM((steps, slab, width), F32),
            pltpu.VMEM((levels - 1, 4, slab, width), F32),
            pltpu.VMEM((slab, width), F32),
            pltpu.VMEM((slab, width), F32),
            pltpu.VMEM((slab, width), F32),
            pltpu.VMEM((lean, width), F32),
            pltpu.VMEM((lean, width), F32),
            pltpu.VMEM((width, width), F32),
            pltpu.VMEM((GROUP - 1, rows, width), F32),
            pltpu.VMEM((far, rows, width), F32),
            pltpu.VMEM((far, rows, width), F32),
            pltpu.VMEM((rows, width), F32),
            pltpu.VMEM((width, width), F32),
            pltpu.VMEM((steps, width), F32),
            dma((levels - 1, 3)), dma((levels - 1, 3)),
            dma((3,)), dma((2,)),
            dma((GROUP - 1,)), dma((GROUP - 1,)),
            dma((far,)), dma((far,)),
            dma((GROUP - 1,)), dma((GROUP - 1,)),
            dma((steps + 2,)),
        ],
        compiler_params=pltpu.CompilerParams(collective_id=0, has_side_effects=True),
    )(gains, offsets, cov_terms)
    return pl.pallas_call(
        hand_over,
        out_shape=shapes,
        in_specs=[vmem] * 3,
        out_specs=(any_space,) * 3,
        scratch_shapes=[dma((3,))],
    )(*results)


def solution(mesh):
    n = mesh.shape["tm"]
    in_specs = (P(("seq", "tm"), None, None), P(("seq", "tm"), None), P(("seq", "tm"), None, None))
    out_specs = (P(("seq", "tm"), None), P(("seq", "tm"), None, None), P("seq", None))
    return jax.shard_map(
        functools.partial(local, n), mesh=mesh, in_specs=in_specs, out_specs=out_specs, check_vma=False
    )
```

time: 39.6 us -> 37 us (0.934)
  local copies, waits for them, and re-layouts: 3.57 us -> 0 us
  Pallas kernels: 35.2 us -> 36.2 us
    unnamed x7 -> x0, local copies, waits for them, and re-layouts: 3.57 us -> none
    pallas_call x1 -> x2, Pallas kernels: 35.2 us -> 36.2 us  [the longest x1 34.6 us: local(): pl.pallas_call(functools.partial(kernel, n), out_shape=shapes, in_specs=[...]
where the time goes in v2:
time: 37 us; the launch traced here: 36.9 us
  Pallas kernels  36.2 us (98%)
  between operations  0.64 us (2%)
    pallas_call x1, Pallas kernels, local(): pl.pallas_call(functools.partial(kernel, n), out_shape=shapes, in_specs=[...  34.6 us
    pallas_call x1, Pallas kernels, local(): pl.pallas_call(hand_over, out_shape=shapes, in_specs=[vmem] * 3, out_spec...  1.69 us

profile of v2, /device:TPU:0, one launch (start us, length us, event | category | flops | bytes accessed | tf_op | source)
XLA Modules:
  0.0 36.9 jit_solution(5794270627682715605)
XLA Ops:
  0.6 34.6 %shard_map.58 = (f32[4,128]{1,0:T(4,128)}, f32[4,128,128]{2,1,0:T(8,128)}, f32[128,128]{1,0:T(8,128)}) custom-call(f32[4,128,128]{2,1,0:T(8,128)} %gains.1, f32[4,128]{1,0:T(4,128)} %offsets.1, f32[4,128,128]{2,1,0:T(8,128)} %covs.1), custom_call_target="tpu_custom_call" | custom-call | tf_op jit(solution)/shard_map/pallas_call | solution.py:265
  35.2 1.7 %shard_map.59 = (f32[4,128]{1,0:T(4,128)}, f32[4,128,128]{2,1,0:T(8,128)}, f32[128,128]{1,0:T(8,128)}) custom-call(f32[4,128]{1,0:T(4,128)} %get-tuple-element.6.a, f32[4,128,128]{2,1,0:T(8,128)} %get-tuple-element.7.b, f32[128,128]{1,0:T(8,128)} %get-tuple-element.8.c), custom_call_target="tpu_custom_call" | custom-call | tf_op jit(solution)/shard_map/pallas_call | solution.py:294
